TPU v7x, 256 devices: a whole 4x4x8 slice. The times are simulated.
256 devices in a mesh: src: 32 (over z_hi, x, core), tgt: 8 (over y, z_lo).
Axes of the slice: x: 4, y: 4, z: 8 (z_hi: 4, z_lo: 2; z = z_hi * 2 + z_lo), core: 2. Of those that a mesh axis runs over, the one named last changes fastest.
Arguments:
- upstream: bfloat16 [256, 128, 324], P('src'), may hold values from -6 to 6
- centers: int32 [2, 256, 128], P(None, 'src'), may hold values from -4 to 259, as said below
- post_relu: bfloat16 [256, 128, 128], P('src'), as said below
- conv_input: bfloat16 [256, 128, 128], P(('src', 'tgt')), may hold values from -6 to 6
- target_feats: bfloat16 [64, 256, 256], P('tgt'), may hold values from -6 to 6
- out_weight: bfloat16 [128, 256], replicated, may hold values from -0.5 to 0.5
- conv_weight: bfloat16 [3, 3, 128, 128], replicated, may hold values from -0.1875 to 0.1875
Outputs:
- tgt_grad: bfloat16 [64, 256, 256], P('tgt', 'src')
- act_grad: bfloat16 [256, 128, 128], P(('src', 'tgt'))
- out_wgrad: float32 [128, 256], replicated
- conv_wgrad: float32 [3, 3, 128, 128], replicated
Inputs may be any that keep to these rules, and one draw needn't show every extreme that they name: centers[0] is a target row from -4 to 67 and centers[1] a target column from -4 to 259; windows may reach outside the target image. `post_relu`: entries are zero or positive.
All inputs are finite; a program needn't handle non-finite values.
Results may differ from a plain program's by a relative error of at most 0.0064.
Values may be sent and summed in bfloat16 or wider, within the bound.
No kernel may reach another device: no remote copies, remote signals or barrier semaphores. Data moves between devices by JAX's collectives and lax.ppermute only.
A program may use at most 64 MiB of HBM per device.

v0:
```python
import math
import jax
import jax.numpy as jnp
from jax import lax
from jax.sharding import PartitionSpec as P


def padded_2(array, sides, width):
    for axis, dim in sides:
        devices, length = (lax.axis_size(axis), array.shape[dim])
        up = [(i, (i + 1) % devices) for i in range(devices - 1)]
        down = [(j, i) for i, j in up]
        last = lax.slice_in_dim(array, length - width, length, axis=dim)
        first = lax.slice_in_dim(array, 0, width, axis=dim)
        before = lax.ppermute(last, axis, up)
        after = lax.ppermute(first, axis, down)
        array = jnp.concatenate([before, array, after], axis=dim)
    return array


def corr_block(center_rows, center_cols, grad_rows, row_start, row_total, col_total):
    source_total = grad_rows.shape[0]
    row_ids = row_start + jnp.arange(row_total, dtype=jnp.int32)
    col_ids = jnp.arange(col_total, dtype=jnp.int32)
    offsets = jnp.arange(9, dtype=jnp.int32)
    row_parts = []
    col_parts = []
    for level_no in range(4):
        level_step = 2**level_no
        row_off = (
            jnp.floor_divide(row_ids, level_step)[None, :]
            - jnp.floor_divide(center_rows, level_step)[:, None]
            + 4
        )
        col_off = (
            jnp.floor_divide(col_ids, level_step)[None, :]
            - jnp.floor_divide(center_cols, level_step)[:, None]
            + 4
        )
        row_hot = jnp.where(
            row_off[:, None, :] == offsets[None, :, None], 0.25**level_no, 0.0
        ).astype(jnp.float32)
        col_hot = jnp.where(col_off[:, None, :] == offsets[None, :, None], 1.0, 0.0).astype(
            jnp.float32
        )
        level_grads = (
            grad_rows[:, 81 * level_no : 81 * (level_no + 1)]
            .astype(jnp.float32)
            .reshape(source_total, 9, 9)
        )
        row_parts.append(row_hot)
        col_parts.append(jnp.einsum("sab,sbx->sax", level_grads, col_hot))
    row_table = jnp.concatenate(row_parts, axis=1)
    col_table = jnp.concatenate(col_parts, axis=1)
    return jnp.einsum("say,sax->syx", row_table, col_table).astype(jnp.bfloat16)


def hidden_grads(src_grad, relu_rows, out_weight):
    hidden = jnp.einsum("rwd,cd->rwc", src_grad, out_weight, preferred_element_type=jnp.float32)
    block_grad = jnp.where(relu_rows > 0, hidden, 0.0).astype(jnp.bfloat16)
    out_term = jnp.einsum("rwc,rwd->cd", relu_rows, src_grad, preferred_element_type=jnp.float32)
    return (block_grad, out_term)


def conv_back(grad_pad, inputs, kernel):
    row_total = inputs.shape[0]
    width_total = inputs.shape[1]
    padded = jnp.pad(grad_pad, ((0, 0), (1, 1), (0, 0)))
    act_sum = jnp.zeros(inputs.shape, jnp.float32)
    tap_grads = []
    for row_tap in range(3):
        for col_tap in range(3):
            window = padded[
                2 - row_tap : 2 - row_tap + row_total, 2 - col_tap : 2 - col_tap + width_total
            ]
            act_sum = act_sum + jnp.einsum(
                "rwo,io->rwi", window, kernel[row_tap, col_tap], preferred_element_type=jnp.float32
            )
            tap_grads.append(
                jnp.einsum("rwi,rwo->io", inputs, window, preferred_element_type=jnp.float32)
            )
    channels = inputs.shape[2]
    return (act_sum, jnp.stack(tap_grads).reshape(3, 3, channels, channels))


def body(upstream, centers, post_relu, conv_input, target_feats, out_weight, conv_weight):
    src_rows, src_width, lookups = upstream.shape
    tgt_rows, tgt_width, feat_width = target_feats.shape
    channels = post_relu.shape[2]
    src_devices = lax.axis_size("src")
    tgt_devices = lax.axis_size("tgt")
    row_first = lax.axis_index("tgt") * tgt_rows
    inv_root = 1.0 / math.sqrt(feat_width)
    source_total = src_rows * src_width
    flat_grads = upstream.reshape(source_total, lookups)
    flat_rows = centers[0].reshape(source_total)
    flat_cols = centers[1].reshape(source_total)
    block_size = math.gcd(256, source_total)

    def build_block(block_no):
        first_row = block_no * block_size
        return corr_block(
            lax.dynamic_slice_in_dim(flat_rows, first_row, block_size),
            lax.dynamic_slice_in_dim(flat_cols, first_row, block_size),
            lax.dynamic_slice_in_dim(flat_grads, first_row, block_size, 0),
            row_first,
            tgt_rows,
            tgt_width,
        )

    corr_grad = lax.map(build_block, jnp.arange(source_total // block_size, dtype=jnp.int32))
    corr_grad = corr_grad.reshape(source_total, tgt_rows, tgt_width)
    corr_flat = corr_grad.reshape(source_total, tgt_rows * tgt_width)
    src_feats = jnp.dot(
        post_relu.reshape(source_total, channels), out_weight, preferred_element_type=jnp.float32
    ).astype(jnp.bfloat16)
    flat_targets = target_feats.reshape(tgt_rows * tgt_width, feat_width)
    corr_piece = lax.slice_in_dim(
        corr_grad, 0, tgt_width // src_devices * lax.axis_size("src"), axis=2
    )
    target_share = lax.psum_scatter(
        jnp.einsum("syc,sd->cyd", corr_piece, src_feats, preferred_element_type=jnp.float32)
        * inv_root,
        "src",
        scatter_dimension=0,
        tiled=True,
    )
    tgt_grad = jnp.transpose(target_share, (1, 0, 2)).astype(jnp.bfloat16)
    tile_rows = src_rows // tgt_devices
    src_partial = jnp.dot(corr_flat, flat_targets, preferred_element_type=jnp.float32) * inv_root
    src_total = lax.psum(src_partial, "tgt")
    src_grad = src_total.reshape(src_rows, src_width, feat_width).astype(jnp.bfloat16)
    block_grad, out_term = hidden_grads(src_grad, post_relu, out_weight)
    grad_pad = padded_2(block_grad, (("src", 0),), 1)
    whole_input = lax.all_gather(conv_input, "tgt", axis=0, tiled=True)
    act_sum, conv_term = conv_back(grad_pad, whole_input, conv_weight)
    out_total, conv_total = lax.psum((out_term, conv_term), "src")
    act_grad = lax.dynamic_slice_in_dim(
        act_sum, lax.axis_index("tgt") * tile_rows, tile_rows, 0
    ).astype(jnp.bfloat16)
    row_count = float(src_rows * src_devices)
    return (tgt_grad, act_grad, out_total / row_count, conv_total / row_count)


def solution(mesh):
    placed = (
        P("src", None, None),
        P(None, "src", None),
        P("src", None, None),
        P(("src", "tgt"), None, None),
        P("tgt", None, None),
        P(),
        P(),
    )
    return jax.shard_map(
        body,
        mesh=mesh,
        in_specs=placed,
        out_specs=(P("tgt", "src", None), P(("src", "tgt"), None, None), P(), P()),
        check_vma=False,
    )
```

profile of v0, /device:TPU:8, one launch (start us, length us, event | category | flops | bytes accessed | tf_op | source)
XLA Modules:
  0.0 605.3 jit_solution(13785077860471548321)
XLA Ops:
  8.0 1.1 pad.23
  9.3 84.5 %while.13 = (s32[]{:T(128)}, bf16[4,256,8,256]{3,2,1,0:T(8,128)(2,1)}, s32[]{:T(128)}, s32[4]{0:T(128)S(1)}, s32[1024]{0:T(1024)S(1)}, /*index=5*/bf16[1024,324]...) while((s32[]{:T(128)}, ...), condition=%wide.region_1.2_spmd, body=%wide.region_0.1_spmd.sunk | while | flops 104745304 | bytes 30385264 | solution.py:111
  11.9 1.0 copy.85
  12.9 2.0 fusion.171
  15.1 1.0 copy.86
  16.1 2.1 fusion.172
  18.3 1.0 copy.88
  19.3 2.0 fusion.174
  21.5 1.0 copy.87
  24.7 5.7 fusion.175
  33.0 1.0 copy.85
  34.0 2.0 fusion.171
  36.2 1.0 copy.86
  37.2 2.1 fusion.172
  39.4 1.0 copy.88
  40.4 2.0 fusion.174
  42.6 1.0 copy.87
  45.9 5.7 fusion.175
  54.1 1.0 copy.85
  55.1 2.0 fusion.171
  57.3 1.0 copy.86
  58.3 2.1 fusion.172
  60.6 1.0 copy.88
  61.6 2.0 fusion.174
  63.8 1.0 copy.87
  67.0 5.7 fusion.175
  75.2 1.0 copy.85
  76.2 2.0 fusion.171
  78.4 1.0 copy.86
  79.4 2.1 fusion.172
  81.7 1.0 copy.88
  82.7 2.0 fusion.174
  84.9 1.0 copy.87
  88.1 5.7 fusion.175
  93.8 3.7 copy.74
  97.5 1.3 convolution_multiply_fusion
  98.8 75.3 %all-reduce.6 = bf16[1024,256]{1,0:T(8,128)(2,1)S(1)} all-reduce(f32[1024,256]{1,0:T(8,128)S(1)} %convolution_multiply_fusion), channel_id=1, replica_groups=mesh['src'=32,'tgt'=8] {'tgt'}, use_global_device_ids=true, to_apply=%region_3.4 | all-reduce | flops 262144 | bytes 1572864 | tf_op jit(solution)/shard_map/psum | solution.py:131
  174.4 1.3 collective-permute-start
  175.7 1.3 collective-permute-start.1
  177.0 1.0 convolution_bitcast_fusion
  178.0 28.5 %all_gather.3 = bf16[8,128,128]{2,1,0:T(8,128)(2,1)S(1)} all-gather(bf16[1,128,128]{2,1,0:T(8,128)(2,1)S(1)} %copy-done.7), channel_id=1, replica_groups=mesh['src'=32,'tgt'=8] {'tgt'}, dimensions={0}, use_global_device_ids=true | all-gather | bytes 294912 | tf_op jit(solution)/shard_map/all_gather | solution.py:135
  209.2 1.1 copy.58
  210.3 5.6 multiply_bitcast_fusion
  215.9 3.1 copy.47
  221.7 280.7 %all-reduce.5.cloned.1.call-done = (f32[128,256]{0,1:T(8,128)}, f32[3,3,128,128]{3,2,1,0:T(8,128)}) async-done(((f32[128,256]{0,1:T(8,128)}, f32[3,3,128,128]{3,2,1,0:T(8,128)}), (f32[128,256]{0,1:T(8,128)}, f32[3,3,128,128]{3,2,1,0:T(8,128)})) %all-reduce.5.cloned.1.call-update) | async-done | bytes 720912 | tf_op jit(solution)/shard_map/psum | solution.py:137
  502.4 0.9 broadcast_multiply_fusion.1
  504.1 1.9 broadcast_multiply_fusion
  506.0 91.0 %reduce-scatter.2.cloned.1.call-done = f32[8,8,256]{2,1,0:T(8,128)} async-done(((f32[256,8,256]{2,1,0:T(8,128)}), f32[8,8,256]{2,1,0:T(8,128)}) %reduce-scatter.2.cloned.1.call-update) | async-done | bytes 65552 | tf_op jit(solution)/shard_map/reduce_scatter | solution.py:121
  (195 shorter events, 26.5 us)
Async XLA Ops:
  7.2 90.3 %copy-start = (bf16[8,256,256]{2,1,0:T(8,128)(2,1)S(1)}, bf16[8,256,256]{2,1,0:T(8,128)(2,1)}, u32[]{:S(2)}) copy-start(bf16[8,256,256]{2,1,0:T(8,128)(2,1)} %param.13) | copy-start | bytes 3145732
  7.2 495.2 %all-reduce.5.cloned.1.call-start = ((), (), s32[]{:S(2)}) async-start(), calls=%async_computation.2 | async-start | bytes 1441792 | tf_op jit(solution)/shard_map/psum | solution.py:137
  9.3 2.5 copy-start.1
  22.5 1.6 copy-start.8
  22.5 2.2 copy-start.9
  24.7 5.7 copy-start.2
  30.4 2.5 copy-start.1
  43.6 1.6 copy-start.8
  43.6 2.2 copy-start.9
  45.9 5.7 copy-start.2
  51.6 2.5 copy-start.1
  64.8 1.6 copy-start.8
  64.8 2.2 copy-start.9
  67.0 5.7 copy-start.2
  72.7 2.5 copy-start.1
  85.9 1.6 copy-start.8
  85.9 2.2 copy-start.9
  88.1 5.7 copy-start.2
  97.5 76.6 %copy-start.3 = (bf16[8,128,128]{2,1,0:T(8,128)(2,1)S(1)}, bf16[8,128,128]{2,1,0:T(8,128)(2,1)}, u32[]{:S(2)}) copy-start(bf16[8,128,128]{2,1,0:T(8,128)(2,1)} %param.11) | copy-start | bytes 786436
  97.5 76.6 %copy-start.5 = (bf16[128,256]{1,0:T(8,128)(2,1)S(1)}, bf16[128,256]{1,0:T(8,128)(2,1)}, u32[]{:S(2)}) copy-start(bf16[128,256]{1,0:T(8,128)(2,1)} %param.14) | copy-start | bytes 196612
  97.5 80.6 %copy-start.7 = (bf16[1,128,128]{2,1,0:T(8,128)(2,1)S(1)}, bf16[1,128,128]{2,1,0:T(8,128)(2,1)}, u32[]{:S(2)}) copy-start(bf16[1,128,128]{2,1,0:T(8,128)(2,1)} %param.12) | copy-start | bytes 98308
  174.4 32.1 %collective-permute-start = (bf16[1,128,128]{2,1,0:T(8,128)(2,1)S(1)}, bf16[1,128,128]{2,1,0:T(8,128)(2,1)S(1)}, u32[]{:S(2)}, u32[]{:S(2)}) collective-permute-start(bf16[1,128,128]{2,1,0:T(8,128)(2,1)S(1)} %get-tuple-element.192), channel_id=1, source_target_pairs={{0,8},{8,16},{16,24},{24,32},{32,40},{40,48},{48,56},{56,64},{64,7... | collective-permute-start | bytes 98312 | tf_op jit(solution)/shard_map/ppermute | solution.py:15
  175.7 30.8 %collective-permute-start.1 = (bf16[1,128,128]{2,1,0:T(8,128)(2,1)S(1)}, bf16[1,128,128]{2,1,0:T(8,128)(2,1)S(1)}, u32[]{:S(2)}, u32[]{:S(2)}) collective-permute-start(bf16[1,128,128]{2,1,0:T(8,128)(2,1)S(1)} %get-tuple-element.193), channel_id=1, source_target_pairs={{8,0},{16,8},{24,16},{32,24},{40,32},{48,40},{56,48},{64,56},{72,6... | collective-permute-start | bytes 98312 | tf_op jit(solution)/shard_map/ppermute | solution.py:16
  206.7 3.6 copy-start.6
  210.2 386.7 %reduce-scatter.2.cloned.1.call-start = ((), (), s32[]{:S(2)}) async-start(), calls=%async_computation.1 | async-start | bytes 2162688 | tf_op jit(solution)/shard_map/reduce_scatter | solution.py:121
  215.9 3.1 copy-start.4
Sparse Core Ops, SparseCore 0:
  210.4 292.0 all-reduce.4
  506.3 90.6 reduce-scatter.1
where the time goes:
time: 606 us; the launch traced here: 605 us
  waiting for transfers between devices  372 us (61%)
  blocking collectives  104 us (17%)
  matrix products  62.9 us (10%)
  local copies, waits for them, and re-layouts  38.5 us (6%)
  between operations  14.3 us (2%)
  other arithmetic  8.06 us (1%)
    psum x1, waiting for transfers between devices, body(): out_total, conv_total = lax.psum((out_term, conv_term), 'src')  281 us
    reduce_scatter x1, waiting for transfers between devices, body(): lax.psum_scatter(jnp.einsum('syc,sd->cyd', corr_piece, src_feats, preferr...  91 us
    psum x1, blocking collectives, body(): src_total = lax.psum(src_partial, 'tgt')  75.3 us
    all_gather x1, blocking collectives, body(): whole_input = lax.all_gather(conv_input, 'tgt', axis=0, tiled=True)  28.5 us
    dot_general x16, matrix products, corr_block(): col_parts.append(jnp.einsum('sab,sbx->sax', level_grads, col_hot))  27.5 us
    dot_general x4, matrix products, corr_block(): return jnp.einsum('say,sax->syx', row_table, col_table).astype(jnp.bfloat16)  22.8 us
    reshape x32, local copies, waits for them, and re-layouts, corr_block(): level_grads = grad_rows[:, 81 * level_no:81 * (level_no + 1)].astype(jnp....  16.4 us
  transfers between devices with their start and end apart: 4, of which 2 were waited for; matrix products, arithmetic and copies ran while one was open for 3% of the time, Pallas kernels for 0%

commit v1 on v0

--- a/solution.py
+++ b/solution.py
@@ -132,7 +132,15 @@
     src_grad = src_total.reshape(src_rows, src_width, feat_width).astype(jnp.bfloat16)
     block_grad, out_term = hidden_grads(src_grad, post_relu, out_weight)
     grad_pad = padded_2(block_grad, (("src", 0),), 1)
-    whole_input = lax.all_gather(conv_input, "tgt", axis=0, tiled=True)
+    whole_input = jnp.concatenate(
+        lax.all_to_all(
+            jnp.stack([conv_input for _ in range(lax.axis_size("tgt"))], axis=0),
+            axis_name="tgt",
+            concat_axis=0,
+            split_axis=0,
+        ),
+        axis=0,
+    )
     act_sum, conv_term = conv_back(grad_pad, whole_input, conv_weight)
     out_total, conv_total = lax.psum((out_term, conv_term), "src")
     act_grad = lax.dynamic_slice_in_dim(

time: 606 us -> 590 us (0.974)
  blocking collectives: 104 us -> 75 us
  starting transfers between devices: 2.66 us -> 8.9 us
    all_gather x1 -> x0, blocking collectives: 28.5 us -> none  [body(): whole_input = lax.all_gather(conv_input, 'tgt', axis=0, tiled=True)]
    all_to_all x0 -> x1, starting transfers between devices: none -> 6.27 us  [body(): lax.all_to_all(jnp.stack([conv_input for _ in range(lax.axis_size('tgt'))...]
  transfers between devices with their start and end apart: 4 -> 5, of which waited for: 2 -> 3; matrix products, arithmetic and copies ran while one was open for 3% -> 17% of each run, Pallas kernels for 0% -> 0%
where the time goes in v1:
time: 590 us; the launch traced here: 589 us
  waiting for transfers between devices  376 us (64%)
  blocking collectives  75 us (13%)
  matrix products  63.9 us (11%)
  local copies, waits for them, and re-layouts  40 us (7%)
  between operations  14.3 us (2%)
  starting transfers between devices  8.9 us (2%)
  other arithmetic  8.07 us (1%)
    psum x1, waiting for transfers between devices, body(): out_total, conv_total = lax.psum((out_term, conv_term), 'src')  282 us
    reduce_scatter x1, waiting for transfers between devices, body(): lax.psum_scatter(jnp.einsum('syc,sd->cyd', corr_piece, src_feats, preferr...  91 us
    psum x1, blocking collectives, body(): src_total = lax.psum(src_partial, 'tgt')  75 us
    dot_general x16, matrix products, corr_block(): col_parts.append(jnp.einsum('sab,sbx->sax', level_grads, col_hot))  27.5 us
    dot_general x4, matrix products, corr_block(): return jnp.einsum('say,sax->syx', row_table, col_table).astype(jnp.bfloat16)  22.8 us
    reshape x32, local copies, waits for them, and re-layouts, corr_block(): level_grads = grad_rows[:, 81 * level_no:81 * (level_no + 1)].astype(jnp....  16.4 us
  transfers between devices with their start and end apart: 5, of which 3 were waited for; matrix products, arithmetic and copies ran while one was open for 17% of the time, Pallas kernels for 0%

profile of v1, /device:TPU:8, one launch (start us, length us, event | category | flops | bytes accessed | tf_op | source)
XLA Modules:
  0.0 589.1 jit_solution(11824357642410044804)
XLA Ops:
  7.2 1.6 stack.41
  8.8 6.3 %all-to-all-start = ((bf16[8,1,128,128]{3,2,1,0:T(8,128)(2,1)}), bf16[8,1,128,128]{3,2,1,0:T(8,128)(2,1)S(1)}, u32[]{:S(2)}, u32[]{:S(2)}) async-start(bf16[8,1,128,128]{3,2,1,0:T(8,128)(2,1)} %stack.41), calls=%async_computation.1 | async-start | bytes 524288 | tf_op jit(solution)/shard_map/all_to_all | solution.py:136
  15.7 1.1 pad.23
  17.0 84.5 %while.13 = (s32[]{:T(128)}, bf16[4,256,8,256]{3,2,1,0:T(8,128)(2,1)}, s32[]{:T(128)}, s32[4]{0:T(128)S(1)}, s32[1024]{0:T(1024)S(1)}, /*index=5*/bf16[1024,324]...) while((s32[]{:T(128)}, ...), condition=%wide.region_1.2_spmd, body=%wide.region_0.1_spmd.sunk | while | flops 104745304 | bytes 30385264 | solution.py:111
  19.6 1.0 copy.85
  20.6 2.0 fusion.171
  22.8 1.0 copy.86
  23.8 2.1 fusion.172
  26.0 1.0 copy.88
  27.0 2.0 fusion.174
  29.2 1.0 copy.87
  32.5 5.7 fusion.175
  40.7 1.0 copy.85
  41.7 2.0 fusion.171
  43.9 1.0 copy.86
  44.9 2.1 fusion.172
  47.1 1.0 copy.88
  48.1 2.0 fusion.174
  50.3 1.0 copy.87
  53.6 5.7 fusion.175
  61.9 1.0 copy.85
  62.9 2.0 fusion.171
  65.1 1.0 copy.86
  66.1 2.1 fusion.172
  68.3 1.0 copy.88
  69.3 2.0 fusion.174
  71.5 1.0 copy.87
  74.7 5.7 fusion.175
  83.0 1.0 copy.85
  84.0 2.0 fusion.171
  86.2 1.0 copy.86
  87.2 2.1 fusion.172
  89.4 1.0 copy.88
  90.4 2.0 fusion.174
  95.8 5.7 fusion.175
  101.5 3.7 copy.74
  105.2 2.3 convolution_multiply_fusion
  107.5 75.0 %all-reduce.6 = bf16[1024,256]{1,0:T(8,128)(2,1)S(1)} all-reduce(f32[1024,256]{1,0:T(8,128)} %convolution_multiply_fusion), channel_id=1, replica_groups=mesh['src'=32,'tgt'=8] {'tgt'}, use_global_device_ids=true, to_apply=%region_3.4 | all-reduce | flops 262144 | bytes 1572864 | tf_op jit(solution)/shard_map/psum | solution.py:131
  182.8 1.3 collective-permute-start
  184.1 1.3 collective-permute-start.1
  185.4 1.0 convolution_bitcast_fusion
  186.4 2.5 collective-permute-done.1
  191.6 1.1 copy.58
  192.7 5.5 multiply_bitcast_fusion
  198.3 3.1 copy.47
  204.1 282.2 %all-reduce.5.cloned.1.call-done = (f32[128,256]{0,1:T(8,128)}, f32[3,3,128,128]{3,2,1,0:T(8,128)}) async-done(((f32[128,256]{0,1:T(8,128)}, f32[3,3,128,128]{3,2,1,0:T(8,128)}), (f32[128,256]{0,1:T(8,128)}, f32[3,3,128,128]{3,2,1,0:T(8,128)})) %all-reduce.5.cloned.1.call-update) | async-done | bytes 720912 | tf_op jit(solution)/shard_map/psum | solution.py:145
  488.0 1.9 broadcast_multiply_fusion
  489.9 91.0 %reduce-scatter.2.cloned.1.call-done = f32[8,8,256]{2,1,0:T(8,128)} async-done(((f32[256,8,256]{2,1,0:T(8,128)}), f32[8,8,256]{2,1,0:T(8,128)}) %reduce-scatter.2.cloned.1.call-update) | async-done | bytes 65552 | tf_op jit(solution)/shard_map/reduce_scatter | solution.py:121
  (193 shorter events, 28.3 us)
Async XLA Ops:
  7.2 98.0 %copy-start = (bf16[8,256,256]{2,1,0:T(8,128)(2,1)S(1)}, bf16[8,256,256]{2,1,0:T(8,128)(2,1)}, u32[]{:S(2)}) copy-start(bf16[8,256,256]{2,1,0:T(8,128)(2,1)} %param.13) | copy-start | bytes 3145732
  8.8 180.3 %all-to-all-start = ((bf16[8,1,128,128]{3,2,1,0:T(8,128)(2,1)}), bf16[8,1,128,128]{3,2,1,0:T(8,128)(2,1)S(1)}, u32[]{:S(2)}, u32[]{:S(2)}) async-start(bf16[8,1,128,128]{3,2,1,0:T(8,128)(2,1)} %stack.41), calls=%async_computation.1 | async-start | bytes 524288 | tf_op jit(solution)/shard_map/all_to_all | solution.py:136
  15.0 471.2 %all-reduce.5.cloned.1.call-start = ((), (), s32[]{:S(2)}) async-start(), calls=%async_computation.3 | async-start | bytes 1441792 | tf_op jit(solution)/shard_map/psum | solution.py:145
  17.0 2.5 copy-start.1
  30.2 1.6 copy-start.6
  30.2 2.2 copy-start.7
  32.5 5.7 copy-start.2
  38.2 2.5 copy-start.1
  51.3 1.6 copy-start.6
  51.4 2.2 copy-start.7
  53.6 5.7 copy-start.2
  59.3 2.5 copy-start.1
  72.5 1.6 copy-start.6
  72.5 2.2 copy-start.7
  74.7 5.7 copy-start.2
  80.4 2.5 copy-start.1
  93.6 1.6 copy-start.6
  93.6 2.2 copy-start.7
  95.8 5.7 copy-start.2
  105.2 77.3 %copy-start.3 = (bf16[8,128,128]{2,1,0:T(8,128)(2,1)S(1)}, bf16[8,128,128]{2,1,0:T(8,128)(2,1)}, u32[]{:S(2)}) copy-start(bf16[8,128,128]{2,1,0:T(8,128)(2,1)} %param.11) | copy-start | bytes 786436
  105.2 77.3 %copy-start.5 = (bf16[128,256]{1,0:T(8,128)(2,1)S(1)}, bf16[128,256]{1,0:T(8,128)(2,1)}, u32[]{:S(2)}) copy-start(bf16[128,256]{1,0:T(8,128)(2,1)} %param.14) | copy-start | bytes 196612
  182.8 3.6 collective-permute-start
  184.1 4.8 collective-permute-start.1
  192.7 388.2 %reduce-scatter.2.cloned.1.call-start = ((), (), s32[]{:S(2)}) async-start(), calls=%async_computation.2 | async-start | bytes 2162688 | tf_op jit(solution)/shard_map/reduce_scatter | solution.py:121
  198.3 3.1 copy-start.4
Sparse Core Ops, SparseCore 0:
  192.8 293.4 all-reduce.4
  490.1 90.6 reduce-scatter.1
